TPU v7x, 32 devices: a whole 2x2x4 slice. The times are simulated.
32 devices in a mesh: groups: 2 (over y), area: 8 (over z, x), row: 2 (over core).
Axes of the slice: x: 2, y: 2, z: 4, core: 2. Of those that a mesh axis runs over, the one named last changes fastest.
Arguments:
- proj_index: int32 [8, 384], P('area', 'row'), may hold values from 0 to 2047
- delays: int32 [8, 2], P('area'), may hold values from 3 to 5
- past_rates: bfloat16 [8, 6, 128, 384], P('area', None, 'groups', 'row'), parts along dimension 2, may hold values from -0.8984375 to 0.8984375
- potential: float32 [8, 128, 4096], P('area', 'groups', 'row'), parts along dimension 1, may hold values from -6 to 6
- stimulus: float32 [8, 128, 4096], P('area', 'groups', 'row'), parts along dimension 1, may hold values from -5 to 5
- leak_rate: float32 [8, 4096], P('area', 'row'), may hold values from 0.1 to 0.6
- recurrence: bfloat16 [8, 4096, 4096], P('area', None, 'row'), may hold values from -0.09375 to 0.09375
- ff_weight: bfloat16 [8, 192, 4096], P('area', None, 'row'), may hold values from -0.4375 to 0.4375
- fb_weight: bfloat16 [8, 192, 4096], P('area', None, 'row'), may hold values from -0.4375 to 0.4375
Outputs:
- final_potential: float32 [8, 128, 4096], P('area', 'groups', 'row'), parts along dimension 1
There are 2 independent parts, one for each index of `groups`. A program takes and returns all parts, laid end to end along the dimension named above; an argument that names none is the same for every part. Nothing has to cross between parts.
Inputs may be any that keep to these rules, and one draw needn't show every extreme that they name: `proj_index`: indices within a block of 2048 neurons.
All inputs are finite; a program needn't handle non-finite values.
Results may differ from a plain program's by a relative error of at most 0.0013.
Values may be sent and summed in bfloat16 or wider, within the bound.
A program may use at most 64 MiB of HBM per device.

v0:
```python
import functools

import jax
import jax.numpy as jnp
from jax import lax
from jax.experimental import pallas as pl
from jax.experimental.pallas import tpu as pltpu
from jax.sharding import PartitionSpec as P

SUB = 3
OUTER = 2
STEPS = SUB * OUTER
WIDTH = 1024
LANES = 128
PAIR = 2
MESH = pl.DeviceIdType.MESH
F32 = jnp.float32
BF16 = jnp.bfloat16


def dot(a, b):
    return jnp.dot(a, b, preferred_element_type=F32)


def kernel(
    areas,
    delays, index, past, potential, stimulus, leak, recurrence, ff, fb,
    out,
    w_own, w_far, ff_w, fb_w, x, stim, leak_v, index_v, acc, own, far, onehot, past_v, proj, hist_a, hist_b,
    in_sems, w_sems, send_sems, recv_sems, ring_send, ring_a, ring_b,
):
    half, lanes = w_own.shape[1:]
    chunks, width = own.shape[1], own.shape[3]
    blocks = half // lanes
    per = width // lanes
    trials = x.shape[0]
    row = lax.axis_index("row")
    area = lax.axis_index("area")
    partner = {"row": 1 - row}
    ahead = {"area": lax.rem(area + 1, areas)}
    behind = {"area": lax.rem(area + areas - 1, areas)}

    barrier = pltpu.get_barrier_semaphore()
    for peer in (partner, ahead, behind):
        pl.semaphore_signal(barrier, inc=1, device_id=peer, device_id_type=MESH)

    def local_copy(source, target, sem):
        copy = pltpu.make_async_copy(source, target, sem)
        copy.start()
        return copy

    get_past = local_copy(past.at[0], past_v, in_sems.at[6])
    get_x = local_copy(potential.at[0], x, in_sems.at[0])
    get_index = local_copy(index, index_v, in_sems.at[1])
    own_row = pl.multiple_of(row * half, half)
    far_row = pl.multiple_of((1 - row) * half, half)
    get_own = [
        local_copy(recurrence.at[0, pl.ds(own_row, half), pl.ds(b * lanes, lanes)], w_own.at[b], w_sems.at[b])
        for b in range(blocks)
    ]
    get_stim = local_copy(stimulus.at[0], stim, in_sems.at[2])
    get_leak = local_copy(leak, leak_v, in_sems.at[3])
    get_far = [
        local_copy(recurrence.at[0, pl.ds(far_row, half), pl.ds(b * lanes, lanes)], w_far.at[b], w_sems.at[blocks + b])
        for b in range(blocks)
    ]
    get_ff = local_copy(ff.at[0], ff_w, in_sems.at[4])
    get_fb = local_copy(fb.at[0], fb_w, in_sems.at[5])

    def send_rates(i, c):
        return pltpu.make_async_remote_copy(
            src_ref=own.at[i, c], dst_ref=far.at[i, c],
            send_sem=send_sems.at[i, c], recv_sem=recv_sems.at[i, c],
            device_id=partner, device_id_type=MESH,
        )

    def send_ring(source, first, count, group):
        slots = pl.ds(first, count)
        return (
            pltpu.make_async_remote_copy(
                src_ref=source, dst_ref=hist_a.at[slots],
                send_sem=ring_send.at[0, group], recv_sem=ring_a.at[group],
                device_id=ahead, device_id_type=MESH,
            ),
            pltpu.make_async_remote_copy(
                src_ref=source, dst_ref=hist_b.at[slots],
                send_sem=ring_send.at[1, group], recv_sem=ring_b.at[group],
                device_id=behind, device_id_type=MESH,
            ),
        )

    def ring_group(g):
        if g == 0:
            return send_ring(past_v.at[pl.ds(1, SUB)], 0, SUB, 0)
        if g < SUB:
            return send_ring(past_v.at[pl.ds(SUB + g, 1)], SUB + g - 1, 1, g)
        return send_ring(proj.at[pl.ds(g - SUB, 1)], SUB + g - 1, 1, g)

    def gather(i):
        total = dot(own[i, 0], onehot[0])
        for c in range(1, chunks):
            total += dot(own[i, c], onehot[c])
        proj[i] = total.astype(BF16)

    def select(hist, i, d):
        return jnp.where(d == SUB, hist[i + 2], jnp.where(d == SUB + 1, hist[i + 1], hist[i]))

    def product(rates, i, weights, c):
        parts = []
        for b in range(c * per, (c + 1) * per, PAIR):
            total = None
            for k in range(chunks):
                rows = slice(k * width, (k + 1) * width)
                tile = jnp.concatenate([weights[b + p, rows] for p in range(PAIR)], axis=1)
                term = dot(rates[i, k], tile)
                total = term if total is None else total + term
            parts.append(total)
        return jnp.concatenate(parts, axis=1)

    get_past.wait()
    pl.semaphore_wait(barrier, 3)
    for copy in ring_group(0):
        copy.start()
    get_x.wait()
    for c in range(chunks):
        own[0, c] = jnp.tanh(x[:, c * width:(c + 1) * width]).astype(BF16)
    get_index.wait()
    for c in range(chunks):
        lanes = index_v[0:1, :]
        spots = lax.broadcasted_iota(jnp.int32, (width, lanes.shape[1]), 0) + c * width
        onehot[c] = jnp.where(spots == lanes, 1.0, 0.0).astype(BF16)
    gather(0)

    for c in range(chunks):
        send_rates(0, c).start()
    for g in range(1, SUB + 1):
        for copy in ring_group(g):
            copy.start()

    for i in range(STEPS):
        first = i == 0
        if 0 < i < SUB:
            gather(i)
            for copy in ring_group(SUB + i):
                copy.start()
        if first:
            get_stim.wait()
            get_leak.wait()
        for c in range(chunks):
            cols = slice(c * width, (c + 1) * width)
            if first:
                for b in range(c * per, (c + 1) * per):
                    get_own[b].wait()
            acc[:, cols] = stim[:, cols] + product(own, i, w_own, c)

        def couple():
            for copy in ring_group(i):
                copy.wait_recv()
            return select(hist_a, i, delays[0, 0]), select(hist_b, i, delays[0, 1])

        if first:
            for c in range(chunks):
                send_rates(0, c).wait_recv()
            for c in range(chunks):
                cols = slice(c * width, (c + 1) * width)
                for b in range(c * per, (c + 1) * per):
                    get_far[b].wait()
                acc[:, cols] += product(far, i, w_far, c)
            get_ff.wait()
            get_fb.wait()
            from_a, from_b = couple()
        else:
            from_a, from_b = couple()
            for c in range(chunks):
                cols = slice(c * width, (c + 1) * width)
                acc[:, cols] += dot(from_a, ff_w[:, cols]) + dot(from_b, fb_w[:, cols])
            for c in range(chunks):
                send_rates(i, c).wait_recv()
        for c in range(chunks):
            cols = slice(c * width, (c + 1) * width)
            if first:
                drive = acc[:, cols] + (dot(from_a, ff_w[:, cols]) + dot(from_b, fb_w[:, cols]))
            else:
                drive = acc[:, cols] + product(far, i, w_far, c)
            now = x[:, cols]
            new = now + leak_v[:, cols] * (drive - now)
            if i + 1 < STEPS:
                x[:, cols] = new
                own[i + 1, c] = jnp.tanh(new).astype(BF16)
                send_rates(i + 1, c).start()
            else:
                out[0, :, cols] = new
    for i in range(STEPS):
        for c in range(chunks):
            send_rates(i, c).wait_send()
        for copy in ring_group(i):
            copy.wait_send()


def local(areas, proj_index, delays, past_rates, potential, stimulus, leak_rate, recurrence, ff_weight, fb_weight):
    _, trials, block = potential.shape
    projecting = proj_index.shape[1]
    width = min(WIDTH, block)
    chunks = block // width
    anywhere = pl.BlockSpec(memory_space=pl.ANY)
    vmem = pltpu.VMEM
    dma = pltpu.SemaphoreType.DMA
    return pl.pallas_call(
        functools.partial(kernel, areas),
        out_shape=vmem(potential.shape, F32),
        in_specs=[pl.BlockSpec(memory_space=pltpu.SMEM)] + [anywhere] * 8,
        out_specs=pl.BlockSpec(memory_space=vmem),
        scratch_shapes=[
            vmem((block // LANES, block, LANES), BF16),
            vmem((block // LANES, block, LANES), BF16),
            vmem(ff_weight.shape[1:], BF16),
            vmem(fb_weight.shape[1:], BF16),
            vmem((trials, block), F32),
            vmem((trials, block), F32),
            vmem((1, block), F32),
            vmem((1, projecting), jnp.int32),
            vmem((trials, block), F32),
            vmem((STEPS, chunks, trials, width), BF16),
            vmem((STEPS, chunks, trials, width), BF16),
            vmem((chunks, width, projecting), BF16),
            vmem(past_rates.shape[1:], BF16),
            vmem((SUB, trials, projecting), BF16),
            vmem((STEPS + 2, trials, projecting), BF16),
            vmem((STEPS + 2, trials, projecting), BF16),
            dma((7,)),
            dma((2 * (block // LANES),)),
            dma((STEPS, chunks)),
            dma((STEPS, chunks)),
            dma((2, STEPS)),
            dma((STEPS,)),
            dma((STEPS,)),
        ],
        compiler_params=pltpu.CompilerParams(
            collective_id=0, has_side_effects=True, vmem_limit_bytes=66_000_000
        ),
        name="loop_dynamics",
    )(delays, *(
        pltpu.with_memory_space_constraint(array, pltpu.HBM)
        for array in (proj_index, past_rates, potential, stimulus, leak_rate, recurrence, ff_weight, fb_weight)
    ))


def solution(mesh):
    return jax.shard_map(
        functools.partial(local, mesh.shape["area"]),
        mesh=mesh,
        in_specs=(
            P("area", "row"),
            P("area", None),
            P("area", None, "groups", "row"),
            P("area", "groups", "row"),
            P("area", "groups", "row"),
            P("area", "row"),
            P("area", None, "row"),
            P("area", None, "row"),
            P("area", None, "row"),
        ),
        out_specs=P("area", "groups", "row"),
        check_vma=False,
    )
```

profile of v0, /device:TPU:0, one launch (start us, length us, event | category | flops | bytes accessed | tf_op | source)
XLA Modules:
  0.0 35.9 jit_solution(9736563618934444591)
XLA Ops:
  0.0 35.1 %loop_dynamics.1 = f32[1,64,2048]{2,1,0:T(8,128)S(1)} custom-call(s32[1,2]{1,0:T(1,128)} %delays.1, s32[1,192]{1,0:T(1,128)} %index.1, bf16[1,6,64,192]{3,2,1,0:T(8,128)(2,1)} %past.1, f32[1,64,2048]{2,1,0:T(8,128)} %potential.1, f32[1,64,2048]{2,1,0:T(8,128)} %stimulus.1, f32[1,2048]{1,0:T(1,128)} %leak.1, bf16[1,4096,2048]{2,1,0:T(8,128)(2,1)} %recurrence.1, ...), custom_call_target="tpu_custom_call" | custom-call | tf_op jit(solution)/shard_map/loop_dynamics/pallas_call | solution.py:208
  35.1 0.8 %copy.11 = f32[1,64,2048]{2,1,0:T(8,128)} copy(f32[1,64,2048]{2,1,0:T(8,128)S(1)} %loop_dynamics.1) | data formatting | bytes 1048576
where the time goes:
time: 36 us; the launch traced here: 35.9 us
  Pallas kernels  35.1 us (98%)
  local copies, waits for them, and re-layouts  0.8 us (2%)
    pallas_call x1, Pallas kernels, local(): pl.pallas_call(functools.partial(kernel, areas), out_shape=vmem(potential...  35.1 us
    unnamed x1, local copies, waits for them, and re-layouts  0.8 us

commit v1 on v0

--- a/solution.py
+++ b/solution.py
@@ -13,6 +13,7 @@
 WIDTH = 1024
 LANES = 128
 PAIR = 2
+GROUP = 4
 MESH = pl.DeviceIdType.MESH
 F32 = jnp.float32
 BF16 = jnp.bfloat16
@@ -26,14 +27,18 @@
     areas,
     delays, index, past, potential, stimulus, leak, recurrence, ff, fb,
     out,
-    w_own, w_far, ff_w, fb_w, x, stim, leak_v, index_v, acc, own, far, onehot, past_v, proj, hist_a, hist_b,
+    w_own, w_far, maps, x, stim, leak_v, index_v, acc, own, far, onehot, past_v, sent, proj, hist_a, hist_b,
     in_sems, w_sems, send_sems, recv_sems, ring_send, ring_a, ring_b,
 ):
     half, lanes = w_own.shape[1:]
     chunks, width = own.shape[1], own.shape[3]
     blocks = half // lanes
     per = width // lanes
+    groups = blocks // GROUP
     trials = x.shape[0]
+    half_trials = trials // 2
+    projecting = index_v.shape[1]
+    rest = projecting - lanes
     row = lax.axis_index("row")
     area = lax.axis_index("area")
     partner = {"row": 1 - row}
@@ -41,7 +46,7 @@
     behind = {"area": lax.rem(area + areas - 1, areas)}
 
     barrier = pltpu.get_barrier_semaphore()
-    for peer in (partner, ahead, behind):
+    for peer in (ahead, behind, partner):
         pl.semaphore_signal(barrier, inc=1, device_id=peer, device_id_type=MESH)
 
     def local_copy(source, target, sem):
@@ -49,23 +54,36 @@
         copy.start()
         return copy
 
-    get_past = local_copy(past.at[0], past_v, in_sems.at[6])
-    get_x = local_copy(potential.at[0], x, in_sems.at[0])
-    get_index = local_copy(index, index_v, in_sems.at[1])
+    get_past = local_copy(past.at[0], past_v, in_sems.at[0])
+    get_x = local_copy(potential.at[0], x, in_sems.at[1])
+    get_index = local_copy(index, index_v, in_sems.at[2])
     own_row = pl.multiple_of(row * half, half)
     far_row = pl.multiple_of((1 - row) * half, half)
-    get_own = [
-        local_copy(recurrence.at[0, pl.ds(own_row, half), pl.ds(b * lanes, lanes)], w_own.at[b], w_sems.at[b])
-        for b in range(blocks)
-    ]
-    get_stim = local_copy(stimulus.at[0], stim, in_sems.at[2])
-    get_leak = local_copy(leak, leak_v, in_sems.at[3])
-    get_far = [
-        local_copy(recurrence.at[0, pl.ds(far_row, half), pl.ds(b * lanes, lanes)], w_far.at[b], w_sems.at[blocks + b])
-        for b in range(blocks)
-    ]
-    get_ff = local_copy(ff.at[0], ff_w, in_sems.at[4])
-    get_fb = local_copy(fb.at[0], fb_w, in_sems.at[5])
+
+    def load_group(target, first_row, g, sem):
+        for b in range(g * GROUP, (g + 1) * GROUP):
+            pltpu.make_async_copy(
+                recurrence.at[0, pl.ds(first_row, half), pl.ds(b * lanes, lanes)], target.at[b], w_sems.at[sem]
+            ).start()
+
+    def wait_group(target, g, sem):
+        slots = target.at[pl.ds(g * GROUP, GROUP)]
+        pltpu.make_async_copy(slots, slots, w_sems.at[sem]).wait()
+
+    for g in range(groups):
+        load_group(w_own, own_row, g, g)
+    get_stim = local_copy(stimulus.at[0], stim, in_sems.at[3])
+    get_leak = local_copy(leak, leak_v, in_sems.at[4])
+
+    def load_maps():
+        for d, weights in enumerate((ff, fb)):
+            pltpu.make_async_copy(weights.at[0], maps.at[d, pl.ds(0, projecting)], in_sems.at[5]).start()
+            pltpu.make_async_copy(
+                weights.at[0, pl.ds(lanes, rest)], maps.at[d, pl.ds(projecting, rest)], in_sems.at[5]
+            ).start()
+
+    def wait_maps():
+        pltpu.make_async_copy(maps, maps, in_sems.at[5]).wait()
 
     def send_rates(i, c):
         return pltpu.make_async_remote_copy(
@@ -91,19 +109,26 @@
 
     def ring_group(g):
         if g == 0:
-            return send_ring(past_v.at[pl.ds(1, SUB)], 0, SUB, 0)
+            return send_ring(sent.at[pl.ds(0, SUB)], 0, SUB, 0)
         if g < SUB:
-            return send_ring(past_v.at[pl.ds(SUB + g, 1)], SUB + g - 1, 1, g)
+            return send_ring(sent.at[pl.ds(SUB + g - 1, 1)], SUB + g - 1, 1, g)
         return send_ring(proj.at[pl.ds(g - SUB, 1)], SUB + g - 1, 1, g)
+
+    low = lax.broadcasted_iota(jnp.int32, (half_trials, lanes), 1) < rest
 
     def gather(i):
         total = dot(own[i, 0], onehot[0])
         for c in range(1, chunks):
             total += dot(own[i, c], onehot[c])
-        proj[i] = total.astype(BF16)
+        tail = total[:, lanes:]
+        proj[i, 0:trials] = total[:, :lanes].astype(BF16)
+        proj[i, trials:] = jnp.where(low, tail[:half_trials], tail[half_trials:]).astype(BF16)
 
     def select(hist, i, d):
-        return jnp.where(d == SUB, hist[i + 2], jnp.where(d == SUB + 1, hist[i + 1], hist[i]))
+        packed = jnp.where(d == SUB, hist[i + 2], jnp.where(d == SUB + 1, hist[i + 1], hist[i]))
+        tail = packed[trials:].astype(F32)
+        tail = jnp.concatenate([jnp.where(low, tail, 0.0), jnp.where(low, 0.0, tail)], axis=0).astype(BF16)
+        return jnp.concatenate([packed[:trials], tail], axis=1)
 
     def product(rates, i, weights, c):
         parts = []
@@ -118,24 +143,30 @@
         return jnp.concatenate(parts, axis=1)
 
     get_past.wait()
+    for s in range(1, STEPS):
+        values = past_v[s].astype(F32)
+        tail = values[:, lanes:]
+        sent[s - 1, 0:trials] = values[:, :lanes].astype(BF16)
+        sent[s - 1, trials:] = jnp.concatenate([tail[:half_trials], tail[half_trials:]], axis=1).astype(BF16)
     pl.semaphore_wait(barrier, 3)
     for copy in ring_group(0):
         copy.start()
     get_x.wait()
     for c in range(chunks):
         own[0, c] = jnp.tanh(x[:, c * width:(c + 1) * width]).astype(BF16)
-    get_index.wait()
-    for c in range(chunks):
-        lanes = index_v[0:1, :]
-        spots = lax.broadcasted_iota(jnp.int32, (width, lanes.shape[1]), 0) + c * width
-        onehot[c] = jnp.where(spots == lanes, 1.0, 0.0).astype(BF16)
-    gather(0)
-
-    for c in range(chunks):
         send_rates(0, c).start()
-    for g in range(1, SUB + 1):
+    for g in range(1, SUB):
         for copy in ring_group(g):
             copy.start()
+    get_index.wait()
+    spread = index_v[0:1, :]
+    spread = jnp.concatenate([spread, spread[:, lanes:]], axis=1)
+    for c in range(chunks):
+        spots = lax.broadcasted_iota(jnp.int32, (width, spread.shape[1]), 0) + c * width
+        onehot[c] = jnp.where(spots == spread, 1.0, 0.0).astype(BF16)
+    gather(0)
+    for copy in ring_group(SUB):
+        copy.start()
 
     for i in range(STEPS):
         first = i == 0
@@ -149,37 +180,44 @@
         for c in range(chunks):
             cols = slice(c * width, (c + 1) * width)
             if first:
-                for b in range(c * per, (c + 1) * per):
-                    get_own[b].wait()
+                for g in range(c * per // GROUP, (c + 1) * per // GROUP):
+                    wait_group(w_own, g, g)
+                    load_group(w_far, far_row, g, groups + g)
+                if c == 0:
+                    load_maps()
             acc[:, cols] = stim[:, cols] + product(own, i, w_own, c)
 
         def couple():
             for copy in ring_group(i):
                 copy.wait_recv()
-            return select(hist_a, i, delays[0, 0]), select(hist_b, i, delays[0, 1])
+            return jnp.concatenate([select(hist_a, i, delays[0, 0]), select(hist_b, i, delays[0, 1])], axis=1)
+
+        def coupled(rates, c):
+            cols = slice(c * width, (c + 1) * width)
+            depth = maps.shape[1]
+            return dot(rates[:, :depth], maps[0, :, cols]) + dot(rates[:, depth:], maps[1, :, cols])
 
         if first:
             for c in range(chunks):
                 send_rates(0, c).wait_recv()
             for c in range(chunks):
                 cols = slice(c * width, (c + 1) * width)
-                for b in range(c * per, (c + 1) * per):
-                    get_far[b].wait()
+                for g in range(c * per // GROUP, (c + 1) * per // GROUP):
+                    wait_group(w_far, g, groups + g)
                 acc[:, cols] += product(far, i, w_far, c)
-            get_ff.wait()
-            get_fb.wait()
-            from_a, from_b = couple()
+            wait_maps()
+            arrived = couple()
         else:
-            from_a, from_b = couple()
+            arrived = couple()
             for c in range(chunks):
                 cols = slice(c * width, (c + 1) * width)
-                acc[:, cols] += dot(from_a, ff_w[:, cols]) + dot(from_b, fb_w[:, cols])
+                acc[:, cols] += coupled(arrived, c)
             for c in range(chunks):
                 send_rates(i, c).wait_recv()
         for c in range(chunks):
             cols = slice(c * width, (c + 1) * width)
             if first:
-                drive = acc[:, cols] + (dot(from_a, ff_w[:, cols]) + dot(from_b, fb_w[:, cols]))
+                drive = acc[:, cols] + coupled(arrived, c)
             else:
                 drive = acc[:, cols] + product(far, i, w_far, c)
             now = x[:, cols]
@@ -202,6 +240,8 @@
     projecting = proj_index.shape[1]
     width = min(WIDTH, block)
     chunks = block // width
+    depth = 2 * projecting - LANES
+    packed = trials + trials // 2
     anywhere = pl.BlockSpec(memory_space=pl.ANY)
     vmem = pltpu.VMEM
     dma = pltpu.SemaphoreType.DMA
@@ -213,8 +253,7 @@
         scratch_shapes=[
             vmem((block // LANES, block, LANES), BF16),
             vmem((block // LANES, block, LANES), BF16),
-            vmem(ff_weight.shape[1:], BF16),
-            vmem(fb_weight.shape[1:], BF16),
+            vmem((2, depth, block), BF16),
             vmem((trials, block), F32),
             vmem((trials, block), F32),
             vmem((1, block), F32),
@@ -222,13 +261,14 @@
             vmem((trials, block), F32),
             vmem((STEPS, chunks, trials, width), BF16),
             vmem((STEPS, chunks, trials, width), BF16),
-            vmem((chunks, width, projecting), BF16),
+            vmem((chunks, width, depth), BF16),
             vmem(past_rates.shape[1:], BF16),
-            vmem((SUB, trials, projecting), BF16),
-            vmem((STEPS + 2, trials, projecting), BF16),
-            vmem((STEPS + 2, trials, projecting), BF16),
-            dma((7,)),
-            dma((2 * (block // LANES),)),
+            vmem((STEPS - 1, packed, LANES), BF16),
+            vmem((SUB, packed, LANES), BF16),
+            vmem((STEPS + 2, packed, LANES), BF16),
+            vmem((STEPS + 2, packed, LANES), BF16),
+            dma((6,)),
+            dma((2 * (block // LANES) // GROUP,)),
             dma((STEPS, chunks)),
             dma((STEPS, chunks)),
             dma((2, STEPS)),

time: 36 us -> 33.4 us (0.928)
  Pallas kernels: 35.1 us -> 32.4 us
    pallas_call x1, Pallas kernels: 35.1 us -> 32.4 us  [local(): pl.pallas_call(functools.partial(kernel, areas), out_shape=vmem(potential...]
where the time goes in v1:
time: 33.4 us; the launch traced here: 33.2 us
  Pallas kernels  32.4 us (97%)
  local copies, waits for them, and re-layouts  0.8 us (2%)
    pallas_call x1, Pallas kernels, local(): pl.pallas_call(functools.partial(kernel, areas), out_shape=vmem(potential...  32.4 us
    unnamed x1, local copies, waits for them, and re-layouts  0.8 us

profile of v1, /device:TPU:0, one launch (start us, length us, event | category | flops | bytes accessed | tf_op | source)
XLA Modules:
  0.0 33.2 jit_solution(8522519647420333730)
XLA Ops:
  0.0 32.4 %loop_dynamics.1 = f32[1,64,2048]{2,1,0:T(8,128)S(1)} custom-call(s32[1,2]{1,0:T(1,128)} %delays.1, s32[1,192]{1,0:T(1,128)} %index.1, bf16[1,6,64,192]{3,2,1,0:T(8,128)(2,1)} %past.1, f32[1,64,2048]{2,1,0:T(8,128)} %potential.1, f32[1,64,2048]{2,1,0:T(8,128)} %stimulus.1, f32[1,2048]{1,0:T(1,128)} %leak.1, bf16[1,4096,2048]{2,1,0:T(8,128)(2,1)} %recurrence.1, ...), custom_call_target="tpu_custom_call" | custom-call | tf_op jit(solution)/shard_map/loop_dynamics/pallas_call | solution.py:248
  32.4 0.8 %copy.11 = f32[1,64,2048]{2,1,0:T(8,128)} copy(f32[1,64,2048]{2,1,0:T(8,128)S(1)} %loop_dynamics.1) | data formatting | bytes 1048576

commit v2 on v1

--- a/solution.py
+++ b/solution.py
@@ -13,14 +13,17 @@
 WIDTH = 1024
 LANES = 128
 PAIR = 2
-GROUP = 4
+ROWS = 128
 MESH = pl.DeviceIdType.MESH
 F32 = jnp.float32
 BF16 = jnp.bfloat16
 
 
 def dot(a, b):
-    return jnp.dot(a, b, preferred_element_type=F32)
+    rows, depth = a.shape
+    if rows < ROWS:
+        a = jnp.concatenate([a, jnp.zeros((ROWS - rows, depth), a.dtype)], axis=0)
+    return jnp.dot(a, b, preferred_element_type=F32)[:rows]
 
 
 def kernel(
@@ -28,13 +31,12 @@
     delays, index, past, potential, stimulus, leak, recurrence, ff, fb,
     out,
     w_own, w_far, maps, x, stim, leak_v, index_v, acc, own, far, onehot, past_v, sent, proj, hist_a, hist_b,
-    in_sems, w_sems, send_sems, recv_sems, ring_send, ring_a, ring_b,
+    in_sems, w_sems, sent_sem, recv_sems, ring_send, ring_recv,
 ):
     half, lanes = w_own.shape[1:]
     chunks, width = own.shape[1], own.shape[3]
     blocks = half // lanes
     per = width // lanes
-    groups = blocks // GROUP
     trials = x.shape[0]
     half_trials = trials // 2
     projecting = index_v.shape[1]
@@ -60,20 +62,17 @@
     own_row = pl.multiple_of(row * half, half)
     far_row = pl.multiple_of((1 - row) * half, half)
 
-    def load_group(target, first_row, g, sem):
-        for b in range(g * GROUP, (g + 1) * GROUP):
+    def load(target, first_row, c, sem):
+        for b in range(c * per, (c + 1) * per):
             pltpu.make_async_copy(
                 recurrence.at[0, pl.ds(first_row, half), pl.ds(b * lanes, lanes)], target.at[b], w_sems.at[sem]
             ).start()
 
-    def wait_group(target, g, sem):
-        slots = target.at[pl.ds(g * GROUP, GROUP)]
-        pltpu.make_async_copy(slots, slots, w_sems.at[sem]).wait()
-
-    for g in range(groups):
-        load_group(w_own, own_row, g, g)
-    get_stim = local_copy(stimulus.at[0], stim, in_sems.at[3])
-    get_leak = local_copy(leak, leak_v, in_sems.at[4])
+    def wait_bytes(ref, sem):
+        pltpu.make_async_copy(ref, ref, sem).wait()
+
+    def loaded(target, c, sem):
+        wait_bytes(target.at[pl.ds(c * per, per)], w_sems.at[sem])
 
     def load_maps():
         for d, weights in enumerate((ff, fb)):
@@ -82,13 +81,10 @@
                 weights.at[0, pl.ds(lanes, rest)], maps.at[d, pl.ds(projecting, rest)], in_sems.at[5]
             ).start()
 
-    def wait_maps():
-        pltpu.make_async_copy(maps, maps, in_sems.at[5]).wait()
-
     def send_rates(i, c):
         return pltpu.make_async_remote_copy(
             src_ref=own.at[i, c], dst_ref=far.at[i, c],
-            send_sem=send_sems.at[i, c], recv_sem=recv_sems.at[i, c],
+            send_sem=sent_sem, recv_sem=recv_sems.at[i],
             device_id=partner, device_id_type=MESH,
         )
 
@@ -97,12 +93,12 @@
         return (
             pltpu.make_async_remote_copy(
                 src_ref=source, dst_ref=hist_a.at[slots],
-                send_sem=ring_send.at[0, group], recv_sem=ring_a.at[group],
+                send_sem=ring_send.at[0], recv_sem=ring_recv.at[group],
                 device_id=ahead, device_id_type=MESH,
             ),
             pltpu.make_async_remote_copy(
                 src_ref=source, dst_ref=hist_b.at[slots],
-                send_sem=ring_send.at[1, group], recv_sem=ring_b.at[group],
+                send_sem=ring_send.at[1], recv_sem=ring_recv.at[group],
                 device_id=behind, device_id_type=MESH,
             ),
         )
@@ -130,7 +126,7 @@
         tail = jnp.concatenate([jnp.where(low, tail, 0.0), jnp.where(low, 0.0, tail)], axis=0).astype(BF16)
         return jnp.concatenate([packed[:trials], tail], axis=1)
 
-    def product(rates, i, weights, c):
+    def product(rates, i, weights, c, arrived=None):
         parts = []
         for b in range(c * per, (c + 1) * per, PAIR):
             total = None
@@ -139,6 +135,8 @@
                 tile = jnp.concatenate([weights[b + p, rows] for p in range(PAIR)], axis=1)
                 term = dot(rates[i, k], tile)
                 total = term if total is None else total + term
+            if arrived is not None:
+                total += coupled(arrived, b)
             parts.append(total)
         return jnp.concatenate(parts, axis=1)
 
@@ -148,6 +146,8 @@
         tail = values[:, lanes:]
         sent[s - 1, 0:trials] = values[:, :lanes].astype(BF16)
         sent[s - 1, trials:] = jnp.concatenate([tail[:half_trials], tail[half_trials:]], axis=1).astype(BF16)
+    for c in range(chunks):
+        load(w_own, own_row, c, c)
     pl.semaphore_wait(barrier, 3)
     for copy in ring_group(0):
         copy.start()
@@ -155,6 +155,9 @@
     for c in range(chunks):
         own[0, c] = jnp.tanh(x[:, c * width:(c + 1) * width]).astype(BF16)
         send_rates(0, c).start()
+    load(w_far, far_row, 0, chunks)
+    get_stim = local_copy(stimulus.at[0], stim, in_sems.at[3])
+    get_leak = local_copy(leak, leak_v, in_sems.at[4])
     for g in range(1, SUB):
         for copy in ring_group(g):
             copy.start()
@@ -168,71 +171,62 @@
     for copy in ring_group(SUB):
         copy.start()
 
-    for i in range(STEPS):
-        first = i == 0
-        if 0 < i < SUB:
+    def couple(i):
+        count = 2 * SUB if i == 0 else 2
+        wait_bytes(hist_a.at[pl.ds(0, count)], ring_recv.at[i])
+        return jnp.concatenate([select(hist_a, i, delays[0, 0]), select(hist_b, i, delays[0, 1])], axis=1)
+
+    def coupled(rates, b):
+        cols = slice(b * lanes, (b + PAIR) * lanes)
+        return dot(rates, jnp.concatenate([maps[d, :, cols] for d in range(2)], axis=0))
+
+    def update(i, c, drive):
+        cols = slice(c * width, (c + 1) * width)
+        now = x[:, cols]
+        new = now + leak_v[:, cols] * (drive - now)
+        if i + 1 < STEPS:
+            x[:, cols] = new
+            own[i + 1, c] = jnp.tanh(new).astype(BF16)
+            send_rates(i + 1, c).start()
+        else:
+            out[0, :, cols] = new
+
+    for c in range(chunks):
+        loaded(w_own, c, c)
+        if c + 1 < chunks:
+            load(w_far, far_row, c + 1, chunks + c + 1)
+        if c == 0:
+            load_maps()
+        acc[:, c * width:(c + 1) * width] = product(own, 0, w_own, c)
+    wait_bytes(far.at[0], recv_sems.at[0])
+    get_stim.wait()
+    get_leak.wait()
+    for c in range(chunks):
+        cols = slice(c * width, (c + 1) * width)
+        loaded(w_far, c, chunks + c)
+        acc[:, cols] += stim[:, cols] + product(far, 0, w_far, c)
+    wait_bytes(maps, in_sems.at[5])
+    arrived = couple(0)
+    for c in range(chunks):
+        terms = [coupled(arrived, b) for b in range(c * per, (c + 1) * per, PAIR)]
+        update(0, c, acc[:, c * width:(c + 1) * width] + jnp.concatenate(terms, axis=1))
+
+    for i in range(1, STEPS):
+        if i < SUB:
             gather(i)
             for copy in ring_group(SUB + i):
                 copy.start()
-        if first:
-            get_stim.wait()
-            get_leak.wait()
         for c in range(chunks):
             cols = slice(c * width, (c + 1) * width)
-            if first:
-                for g in range(c * per // GROUP, (c + 1) * per // GROUP):
-                    wait_group(w_own, g, g)
-                    load_group(w_far, far_row, g, groups + g)
-                if c == 0:
-                    load_maps()
             acc[:, cols] = stim[:, cols] + product(own, i, w_own, c)
-
-        def couple():
-            for copy in ring_group(i):
-                copy.wait_recv()
-            return jnp.concatenate([select(hist_a, i, delays[0, 0]), select(hist_b, i, delays[0, 1])], axis=1)
-
-        def coupled(rates, c):
-            cols = slice(c * width, (c + 1) * width)
-            depth = maps.shape[1]
-            return dot(rates[:, :depth], maps[0, :, cols]) + dot(rates[:, depth:], maps[1, :, cols])
-
-        if first:
-            for c in range(chunks):
-                send_rates(0, c).wait_recv()
-            for c in range(chunks):
-                cols = slice(c * width, (c + 1) * width)
-                for g in range(c * per // GROUP, (c + 1) * per // GROUP):
-                    wait_group(w_far, g, groups + g)
-                acc[:, cols] += product(far, i, w_far, c)
-            wait_maps()
-            arrived = couple()
-        else:
-            arrived = couple()
-            for c in range(chunks):
-                cols = slice(c * width, (c + 1) * width)
-                acc[:, cols] += coupled(arrived, c)
-            for c in range(chunks):
-                send_rates(i, c).wait_recv()
+        arrived = couple(i)
+        wait_bytes(far.at[i], recv_sems.at[i])
         for c in range(chunks):
             cols = slice(c * width, (c + 1) * width)
-            if first:
-                drive = acc[:, cols] + coupled(arrived, c)
-            else:
-                drive = acc[:, cols] + product(far, i, w_far, c)
-            now = x[:, cols]
-            new = now + leak_v[:, cols] * (drive - now)
-            if i + 1 < STEPS:
-                x[:, cols] = new
-                own[i + 1, c] = jnp.tanh(new).astype(BF16)
-                send_rates(i + 1, c).start()
-            else:
-                out[0, :, cols] = new
-    for i in range(STEPS):
-        for c in range(chunks):
-            send_rates(i, c).wait_send()
-        for copy in ring_group(i):
-            copy.wait_send()
+            update(i, c, acc[:, cols] + product(far, i, w_far, c, arrived))
+    wait_bytes(own, sent_sem)
+    wait_bytes(hist_a, ring_send.at[0])
+    wait_bytes(hist_b, ring_send.at[1])
 
 
 def local(areas, proj_index, delays, past_rates, potential, stimulus, leak_rate, recurrence, ff_weight, fb_weight):
@@ -268,11 +262,10 @@
             vmem((STEPS + 2, packed, LANES), BF16),
             vmem((STEPS + 2, packed, LANES), BF16),
             dma((6,)),
-            dma((2 * (block // LANES) // GROUP,)),
-            dma((STEPS, chunks)),
-            dma((STEPS, chunks)),
-            dma((2, STEPS)),
+            dma((2 * chunks,)),
+            dma,
             dma((STEPS,)),
+            dma((2,)),
             dma((STEPS,)),
         ],
         compiler_params=pltpu.CompilerParams(

time: 33.4 us -> 29.8 us (0.89)
  Pallas kernels: 32.4 us -> 28.8 us
    pallas_call x1, Pallas kernels: 32.4 us -> 28.8 us  [local(): pl.pallas_call(functools.partial(kernel, areas), out_shape=vmem(potential...]
where the time goes in v2:
time: 29.8 us; the launch traced here: 29.6 us
  Pallas kernels  28.8 us (97%)
  local copies, waits for them, and re-layouts  0.8 us (3%)
    pallas_call x1, Pallas kernels, local(): pl.pallas_call(functools.partial(kernel, areas), out_shape=vmem(potential...  28.8 us
    unnamed x1, local copies, waits for them, and re-layouts  0.8 us

profile of v2, /device:TPU:0, one launch (start us, length us, event | category | flops | bytes accessed | tf_op | source)
XLA Modules:
  0.0 29.6 jit_solution(11031614885241060695)
XLA Ops:
  0.0 28.8 %loop_dynamics.1 = f32[1,64,2048]{2,1,0:T(8,128)S(1)} custom-call(s32[1,2]{1,0:T(1,128)} %delays.1, s32[1,192]{1,0:T(1,128)} %index.1, bf16[1,6,64,192]{3,2,1,0:T(8,128)(2,1)} %past.1, f32[1,64,2048]{2,1,0:T(8,128)} %potential.1, f32[1,64,2048]{2,1,0:T(8,128)} %stimulus.1, f32[1,2048]{1,0:T(1,128)} %leak.1, bf16[1,4096,2048]{2,1,0:T(8,128)(2,1)} %recurrence.1, ...), custom_call_target="tpu_custom_call" | custom-call | tf_op jit(solution)/shard_map/loop_dynamics/pallas_call | solution.py:242
  28.8 0.8 %copy.11 = f32[1,64,2048]{2,1,0:T(8,128)} copy(f32[1,64,2048]{2,1,0:T(8,128)S(1)} %loop_dynamics.1) | data formatting | bytes 1048576

commit v3 on v2

--- a/solution.py
+++ b/solution.py
@@ -28,9 +28,9 @@
 
 def kernel(
     areas,
-    delays, index, past, potential, stimulus, leak, recurrence, ff, fb,
+    delays_in, index, past, potential, stimulus, leak, recurrence, ff, fb,
     out,
-    w_own, w_far, maps, x, stim, leak_v, index_v, acc, own, far, onehot, past_v, sent, proj, hist_a, hist_b,
+    w_own, w_far, maps, x, stim, leak_v, index_v, acc, own, far, onehot, delays, past_v, sent, proj, hist_a, hist_b,
     in_sems, w_sems, sent_sem, recv_sems, ring_send, ring_recv,
 ):
     half, lanes = w_own.shape[1:]
@@ -59,6 +59,7 @@
     get_past = local_copy(past.at[0], past_v, in_sems.at[0])
     get_x = local_copy(potential.at[0], x, in_sems.at[1])
     get_index = local_copy(index, index_v, in_sems.at[2])
+    get_delays = local_copy(delays_in, delays, in_sems.at[6])
     own_row = pl.multiple_of(row * half, half)
     far_row = pl.multiple_of((1 - row) * half, half)
 
@@ -126,19 +127,18 @@
         tail = jnp.concatenate([jnp.where(low, tail, 0.0), jnp.where(low, 0.0, tail)], axis=0).astype(BF16)
         return jnp.concatenate([packed[:trials], tail], axis=1)
 
-    def product(rates, i, weights, c, arrived=None):
-        parts = []
+    def product(rates, i, weights, b):
+        total = None
+        for k in range(chunks):
+            rows = slice(k * width, (k + 1) * width)
+            tile = jnp.concatenate([weights[b + p, rows] for p in range(PAIR)], axis=1)
+            term = dot(rates[i, k], tile)
+            total = term if total is None else total + term
+        return total
+
+    def pairs(c):
         for b in range(c * per, (c + 1) * per, PAIR):
-            total = None
-            for k in range(chunks):
-                rows = slice(k * width, (k + 1) * width)
-                tile = jnp.concatenate([weights[b + p, rows] for p in range(PAIR)], axis=1)
-                term = dot(rates[i, k], tile)
-                total = term if total is None else total + term
-            if arrived is not None:
-                total += coupled(arrived, b)
-            parts.append(total)
-        return jnp.concatenate(parts, axis=1)
+            yield b, slice(b * lanes, (b + PAIR) * lanes)
 
     get_past.wait()
     for s in range(1, STEPS):
@@ -148,6 +148,9 @@
         sent[s - 1, trials:] = jnp.concatenate([tail[:half_trials], tail[half_trials:]], axis=1).astype(BF16)
     for c in range(chunks):
         load(w_own, own_row, c, c)
+    get_stim = local_copy(stimulus.at[0], stim, in_sems.at[3])
+    get_leak = local_copy(leak, leak_v, in_sems.at[4])
+    load(w_far, far_row, 0, chunks)
     pl.semaphore_wait(barrier, 3)
     for copy in ring_group(0):
         copy.start()
@@ -155,12 +158,33 @@
     for c in range(chunks):
         own[0, c] = jnp.tanh(x[:, c * width:(c + 1) * width]).astype(BF16)
         send_rates(0, c).start()
-    load(w_far, far_row, 0, chunks)
-    get_stim = local_copy(stimulus.at[0], stim, in_sems.at[3])
-    get_leak = local_copy(leak, leak_v, in_sems.at[4])
+    for c in range(1, chunks):
+        load(w_far, far_row, c, chunks + c)
+    load_maps()
     for g in range(1, SUB):
         for copy in ring_group(g):
             copy.start()
+    def couple(i):
+        count = 2 * SUB if i == 0 else 2
+        wait_bytes(hist_a.at[pl.ds(0, count)], ring_recv.at[i])
+        return jnp.concatenate([select(hist_a, i, delays[0, 0]), select(hist_b, i, delays[0, 1])], axis=1)
+
+    def coupled(rates, cols):
+        return dot(rates, jnp.concatenate([maps[d, :, cols] for d in range(2)], axis=0))
+
+    def update(i, c, cols, drive):
+        now = x[:, cols]
+        new = now + leak_v[:, cols] * (drive - now)
+        if i + 1 < STEPS:
+            x[:, cols] = new
+            own[i + 1, c, :, cols.start - c * width:cols.stop - c * width] = jnp.tanh(new).astype(BF16)
+        else:
+            out[0, :, cols] = new
+
+    for c in range(chunks):
+        loaded(w_own, c, c)
+        for b, cols in pairs(c):
+            acc[:, cols] = product(own, 0, w_own, b)
     get_index.wait()
     spread = index_v[0:1, :]
     spread = jnp.concatenate([spread, spread[:, lanes:]], axis=1)
@@ -170,46 +194,20 @@
     gather(0)
     for copy in ring_group(SUB):
         copy.start()
-
-    def couple(i):
-        count = 2 * SUB if i == 0 else 2
-        wait_bytes(hist_a.at[pl.ds(0, count)], ring_recv.at[i])
-        return jnp.concatenate([select(hist_a, i, delays[0, 0]), select(hist_b, i, delays[0, 1])], axis=1)
-
-    def coupled(rates, b):
-        cols = slice(b * lanes, (b + PAIR) * lanes)
-        return dot(rates, jnp.concatenate([maps[d, :, cols] for d in range(2)], axis=0))
-
-    def update(i, c, drive):
-        cols = slice(c * width, (c + 1) * width)
-        now = x[:, cols]
-        new = now + leak_v[:, cols] * (drive - now)
-        if i + 1 < STEPS:
-            x[:, cols] = new
-            own[i + 1, c] = jnp.tanh(new).astype(BF16)
-            send_rates(i + 1, c).start()
-        else:
-            out[0, :, cols] = new
-
-    for c in range(chunks):
-        loaded(w_own, c, c)
-        if c + 1 < chunks:
-            load(w_far, far_row, c + 1, chunks + c + 1)
-        if c == 0:
-            load_maps()
-        acc[:, c * width:(c + 1) * width] = product(own, 0, w_own, c)
     wait_bytes(far.at[0], recv_sems.at[0])
     get_stim.wait()
     get_leak.wait()
     for c in range(chunks):
-        cols = slice(c * width, (c + 1) * width)
         loaded(w_far, c, chunks + c)
-        acc[:, cols] += stim[:, cols] + product(far, 0, w_far, c)
+        for b, cols in pairs(c):
+            acc[:, cols] += stim[:, cols] + product(far, 0, w_far, b)
     wait_bytes(maps, in_sems.at[5])
+    get_delays.wait()
     arrived = couple(0)
     for c in range(chunks):
-        terms = [coupled(arrived, b) for b in range(c * per, (c + 1) * per, PAIR)]
-        update(0, c, acc[:, c * width:(c + 1) * width] + jnp.concatenate(terms, axis=1))
+        for b, cols in pairs(c):
+            update(0, c, cols, acc[:, cols] + coupled(arrived, cols))
+        send_rates(1, c).start()
 
     for i in range(1, STEPS):
         if i < SUB:
@@ -217,13 +215,15 @@
             for copy in ring_group(SUB + i):
                 copy.start()
         for c in range(chunks):
-            cols = slice(c * width, (c + 1) * width)
-            acc[:, cols] = stim[:, cols] + product(own, i, w_own, c)
+            for b, cols in pairs(c):
+                acc[:, cols] = stim[:, cols] + product(own, i, w_own, b)
         arrived = couple(i)
         wait_bytes(far.at[i], recv_sems.at[i])
         for c in range(chunks):
-            cols = slice(c * width, (c + 1) * width)
-            update(i, c, acc[:, cols] + product(far, i, w_far, c, arrived))
+            for b, cols in pairs(c):
+                update(i, c, cols, acc[:, cols] + product(far, i, w_far, b) + coupled(arrived, cols))
+            if i + 1 < STEPS:
+                send_rates(i + 1, c).start()
     wait_bytes(own, sent_sem)
     wait_bytes(hist_a, ring_send.at[0])
     wait_bytes(hist_b, ring_send.at[1])
@@ -242,7 +242,7 @@
     return pl.pallas_call(
         functools.partial(kernel, areas),
         out_shape=vmem(potential.shape, F32),
-        in_specs=[pl.BlockSpec(memory_space=pltpu.SMEM)] + [anywhere] * 8,
+        in_specs=[anywhere] * 9,
         out_specs=pl.BlockSpec(memory_space=vmem),
         scratch_shapes=[
             vmem((block // LANES, block, LANES), BF16),
@@ -256,12 +256,13 @@
             vmem((STEPS, chunks, trials, width), BF16),
             vmem((STEPS, chunks, trials, width), BF16),
             vmem((chunks, width, depth), BF16),
+            pltpu.SMEM(delays.shape, jnp.int32),
             vmem(past_rates.shape[1:], BF16),
             vmem((STEPS - 1, packed, LANES), BF16),
             vmem((SUB, packed, LANES), BF16),
             vmem((STEPS + 2, packed, LANES), BF16),
             vmem((STEPS + 2, packed, LANES), BF16),
-            dma((6,)),
+            dma((7,)),
             dma((2 * chunks,)),
             dma,
             dma((STEPS,)),
@@ -272,9 +273,9 @@
             collective_id=0, has_side_effects=True, vmem_limit_bytes=66_000_000
         ),
         name="loop_dynamics",
-    )(delays, *(
+    )(*(
         pltpu.with_memory_space_constraint(array, pltpu.HBM)
-        for array in (proj_index, past_rates, potential, stimulus, leak_rate, recurrence, ff_weight, fb_weight)
+        for array in (delays, proj_index, past_rates, potential, stimulus, leak_rate, recurrence, ff_weight, fb_weight)
     ))
 
 

time: 29.8 us -> 27.7 us (0.930)
  Pallas kernels: 28.8 us -> 26.8 us
    pallas_call x1, Pallas kernels: 28.8 us -> 26.8 us  [local(): pl.pallas_call(functools.partial(kernel, areas), out_shape=vmem(potential...]
where the time goes in v3:
time: 27.7 us; the launch traced here: 27.6 us
  Pallas kernels  26.8 us (97%)
  local copies, waits for them, and re-layouts  0.8 us (3%)
    pallas_call x1, Pallas kernels, local(): pl.pallas_call(functools.partial(kernel, areas), out_shape=vmem(potential...  26.8 us
    unnamed x1, local copies, waits for them, and re-layouts  0.8 us

profile of v3, /device:TPU:0, one launch (start us, length us, event | category | flops | bytes accessed | tf_op | source)
XLA Modules:
  0.0 27.6 jit_solution(1675940321902671809)
XLA Ops:
  0.0 26.8 %loop_dynamics.1 = f32[1,64,2048]{2,1,0:T(8,128)S(1)} custom-call(s32[1,2]{1,0:T(1,128)} %delays_in.1, s32[1,192]{1,0:T(1,128)} %index.1, bf16[1,6,64,192]{3,2,1,0:T(8,128)(2,1)} %past.1, f32[1,64,2048]{2,1,0:T(8,128)} %potential.1, f32[1,64,2048]{2,1,0:T(8,128)} %stimulus.1, f32[1,2048]{1,0:T(1,128)} %leak.1, bf16[1,4096,2048]{2,1,0:T(8,128)(2,1)} %recurrence.1, ...), custom_call_target="tpu_custom_call" | custom-call | tf_op jit(solution)/shard_map/loop_dynamics/pallas_call | solution.py:242
  26.8 0.8 %copy.11 = f32[1,64,2048]{2,1,0:T(8,128)} copy(f32[1,64,2048]{2,1,0:T(8,128)S(1)} %loop_dynamics.1) | data formatting | bytes 1048576
